TPU v7x, 128 devices: a whole 4x4x4 slice. The times are simulated.
128 devices in a mesh: inp: 8 (over z, x_hi), tm: 8 (over x_lo, y), bl: 2 (over core).
Axes of the slice: x: 4 (x_hi: 2, x_lo: 2; x = x_hi * 2 + x_lo), y: 4, z: 4, core: 2. Of those that a mesh axis runs over, the one named last changes fastest.
Arguments:
- voltages: int32 [1024, 524288], P(('inp', 'bl'), 'tm'), may hold values from -16 to 14, as said below
- taps: float32 [4, 16384], replicated, may hold values from -3 to 3
- flags: int32 [1024], P(('inp', 'bl')), may hold values 0 or 1
Outputs:
- visibilities: float32 [2, 128, 8, 128, 1024], P(None, ('inp', 'tm'), None, 'bl')
Inputs may be any that keep to these rules, and one draw needn't show every extreme that they name: `voltages`: int8-valued digitized samples, each input's stream in time order.
All inputs are finite; a program needn't handle non-finite values. No bound on the sum of `flags` on one device may be relied on, other than what follows from the above.
Results may differ from a plain program's by a relative error of at most 0.00065.
Values may be sent and summed in bfloat16 or wider, within the bound.
A program may use at most 192 MiB of HBM per device.

v0:
```python
import math
import jax
import jax.numpy as jnp
from jax import lax
from jax.sharding import PartitionSpec as P

CH_AVG = 64
FIRST = 128


def passed_along(value, axis, steps):
    count = lax.axis_size(axis)
    initial, last = (max(0, -steps), min(count, count - steps))
    return lax.ppermute(value, axis, [(source, source + steps) for source in range(initial, last)])


def cos_sin(height, breadth, period):
    grid = lax.broadcasted_iota(jnp.int32, (height, breadth), 0) * lax.broadcasted_iota(
        jnp.int32, (height, breadth), 1
    )
    angle = (grid % period).astype(jnp.float32) * (2.0 * math.pi / period)
    return (jnp.cos(angle), jnp.sin(angle))


def transform(blocks, length, precision):
    first_len = FIRST
    second_len = length // first_len
    highs = length // 2 // first_len
    cos_one, sin_one = cos_sin(first_len, first_len, first_len)
    table_one = jnp.stack([cos_one, -sin_one])
    section_one = jnp.einsum("xca,mab->xmcb", table_one, blocks, precision=precision)
    cos_twist, sin_twist = cos_sin(first_len, second_len, length)
    real_one = section_one[0]
    imag_one = section_one[1]
    twisted = jnp.stack(
        [real_one * cos_twist + imag_one * sin_twist, imag_one * cos_twist - real_one * sin_twist]
    )
    cos_two, sin_two = cos_sin(highs, second_len, second_len)
    table_two = jnp.stack(
        [jnp.stack([cos_two, sin_two], axis=1), jnp.stack([-sin_two, cos_two], axis=1)]
    )
    return jnp.einsum("yqxb,xmcb->yqmc", table_two, twisted, precision=precision)


def shards(voltages, taps, flags):
    inputs = voltages.shape[0]
    tap_count = taps.shape[0]
    length = taps.shape[1]
    second_len = length // FIRST
    spectra_dev = voltages.shape[1] // length
    reach = tap_count - 1
    local = spectra_dev - reach
    precision = lax.Precision.HIGH
    blocked = voltages.reshape(inputs, spectra_dev, FIRST, second_len)
    leading = blocked[:, :reach].astype(jnp.bfloat16)
    following = passed_along(leading, "tm", -1)
    samples = blocked.astype(jnp.float32)
    tap_blocks = taps.reshape(tap_count, FIRST, second_len)

    def filtered(pieces, count):
        rows = []
        for spectrum in range(count):
            total = jnp.zeros((inputs, FIRST, second_len), jnp.float32)
            for offset in range(tap_count):
                total = total + tap_blocks[offset][None] * pieces[spectrum + offset]
            rows.append(total)
        return jnp.concatenate(rows, axis=0)

    own_pieces = [samples[:, j] for j in range(spectra_dev)]
    next_pieces = [following[:, j].astype(jnp.float32) for j in range(reach)]
    first_part = transform(filtered(own_pieces, local), length, precision)
    second_part = transform(filtered(own_pieces[local:] + next_pieces, reach), length, precision)
    both_parts = jnp.concatenate([first_part, second_part], axis=2)
    scale = jnp.tile(flags.astype(jnp.float32) / (8.0 * math.sqrt(length)), spectra_dev)
    spectra = (both_parts * scale[None, None, :, None]).astype(jnp.bfloat16)
    turned = lax.all_to_all(spectra, ("inp", "tm"), split_axis=1, concat_axis=1, tiled=True)
    groups_inp = lax.axis_size("inp")
    groups_tm = lax.axis_size("tm")
    out_groups = FIRST // CH_AVG
    rows = turned.reshape(2, groups_inp, groups_tm, spectra_dev, inputs, FIRST)
    own = jnp.transpose(rows, (1, 4, 0, 2, 3, 5)).reshape(groups_inp, inputs, -1)
    half = own.shape[-1] // 2
    swapped = jnp.concatenate([own[..., half:], -own[..., :half]], axis=-1)
    lane_group = lax.broadcasted_iota(jnp.int32, (out_groups, own.shape[-1]), 1) % FIRST // CH_AVG
    mask = lane_group == lax.broadcasted_iota(jnp.int32, (out_groups, own.shape[-1]), 0)
    mask = mask.astype(own.dtype)
    lhs = jnp.stack([own, swapped])[:, None] * mask[None, :, None, None, :]
    columns = lax.all_gather(own, "bl", axis=1, tiled=True).reshape(-1, own.shape[-1])
    count = float(groups_tm * spectra_dev * CH_AVG)
    products = jnp.einsum("xgpik,qk->xgpiq", lhs, columns, preferred_element_type=jnp.float32)
    return products * (1.0 / count)


def solution(mesh):
    in_specs = (P(("inp", "bl"), "tm"), P(), P(("inp", "bl")))
    out_specs = P(None, ("inp", "tm"), None, "bl", None)
    return jax.shard_map(shards, mesh=mesh, in_specs=in_specs, out_specs=out_specs, check_vma=False)
```

profile of v0, /device:TPU:2, one launch (start us, length us, event | category | flops | bytes accessed | tf_op | source)
XLA Modules:
  0.0 504.2 jit_solution(362682598263856912)
XLA Ops:
  6.5 21.8 %convert_bitcast_fusion.1 = (bf16[8,8,512,128]{3,1,2,0:T(8,128)(2,1)}, f32[8,8,512,128]{3,1,2,0:T(8,128)}) fusion(s32[64,65536]{1,0:T(8,128)} %param.3), kind=kLoop, calls=%fused_computation.27 | loop fusion | flops 8388608 | bytes 41943040
  28.3 9.0 %copy.51 = bf16[8,8,512,128]{3,2,1,0:T(8,128)(2,1)} copy(bf16[8,8,512,128]{3,1,2,0:T(8,128)(2,1)} %get-tuple-element.11) | data formatting | bytes 16777216
  37.3 8.1 %slice.95 = bf16[64,3,128,128]{3,2,1,0:T(8,128)(2,1)} slice(bf16[64,4,128,128]{3,2,1,0:T(8,128)(2,1)} %bitcast.155), slice={[0:64], [0:3], [0:128], [0:128]} | slice | bytes 12582912 | tf_op jit(solution)/shard_map/slice | solution.py:55
  45.4 8.6 %copy.49 = bf16[64,3,128,128]{2,3,0,1:T(8,128)(2,1)} copy(bf16[64,3,128,128]{3,2,1,0:T(8,128)(2,1)} %slice.95) | data formatting | bytes 12582912
  54.0 5.2 %collective-permute-start = (bf16[64,3,128,128]{2,3,0,1:T(8,128)(2,1)}, bf16[64,3,128,128]{2,3,0,1:T(8,128)(2,1)}, u32[]{:S(2)}, u32[]{:S(2)}) collective-permute-start(bf16[64,3,128,128]{2,3,0,1:T(8,128)(2,1)} %copy.49), channel_id=1, source_target_pairs={{2,0},{4,2},{6,4},{8,6},{10,8},{12,10},{14,12},{3,1},{5,3},{7,5},{... | collective-permute-start | bytes 18874376 | tf_op jit(solution)/shard_map/ppermute | solution.py:14
  59.2 9.4 %copy.50 = f32[8,8,512,128]{3,2,1,0:T(8,128)S(1)} copy(f32[8,8,512,128]{3,1,2,0:T(8,128)} %get-tuple-element.12) | data formatting | bytes 33554432
  68.6 6.0 %fusion.77 = (f32[64,1,128,128]{3,2,1,0:T(8,128)}, f32[64,1,128,128]{3,2,1,0:T(8,128)}, f32[64,1,128,128]{3,2,1,0:T(8,128)}, f32[64,1,128,128]{3,2,1,0:T(8,128)}) fusion(f32[64,4,128,128]{3,2,1,0:T(8,128)S(1)} %bitcast.153), kind=kLoop, calls=%fused_computation.128 | loop fusion | bytes 33554432 | tf_op jit(solution)/shard_map/slice | solution.py:69
  74.6 5.6 %copy.46 = f32[64,1,128,128]{2,3,0,1:T(8,128)} copy(f32[64,1,128,128]{3,2,1,0:T(8,128)} %get-tuple-element.9) | data formatting | bytes 8388608
  80.3 5.7 %copy.47 = f32[64,1,128,128]{2,3,0,1:T(8,128)} copy(f32[64,1,128,128]{3,2,1,0:T(8,128)} %get-tuple-element.8) | data formatting | bytes 8388608
  85.9 5.6 %copy.48 = f32[64,1,128,128]{2,3,0,1:T(8,128)} copy(f32[64,1,128,128]{3,2,1,0:T(8,128)} %get-tuple-element.10) | data formatting | bytes 8388608
  91.5 5.6 %copy.45 = f32[64,1,128,128]{2,3,0,1:T(8,128)} copy(f32[64,1,128,128]{3,2,1,0:T(8,128)} %get-tuple-element.7) | data formatting | bytes 8388608
  98.2 0.3 sine_negate_fusion
  98.5 0.3 fusion.63
  98.8 8.0 %fusion.37 = f32[2,64,128,128]{2,3,0,1:T(8,128)S(1)} fusion(f32[64,1,128,128]{2,3,0,1:T(8,128)} %copy.48, f32[64,1,128,128]{2,3,0,1:T(8,128)} %copy.47, f32[64,1,128,128]{2,3,0,1:T(8,128)} %copy.46, f32[64,1,128,128]{2,3,0,1:T(8,128)} %copy.45, f32[128,128]{0,1:T(8,128)S(1)} %copy.28, f32[128,128]{0,1:T(8,128)S(1)} %copy.26, f32[128,128]{0,1:T(8,128)S(1)} %copy.24, ...), kind=kOutput, calls=%fused_computation.63 | convolution fusion | flops 1617985536 | bytes 25559040 | tf_op jit(solution)/shard_map/xca,mab->xmcb/dot_general | solution.py:31
  106.7 1.2 multiply_add_fusion.1
  108.0 4.4 fusion.40
  112.3 81.6 %collective-permute-done = bf16[64,3,128,128]{2,3,0,1:T(8,128)(2,1)} collective-permute-done((bf16[64,3,128,128]{2,3,0,1:T(8,128)(2,1)}, bf16[64,3,128,128]{2,3,0,1:T(8,128)(2,1)}, u32[]{:S(2)}, u32[]{:S(2)}) %collective-permute-start) | collective-permute-done | bytes 6291488 | tf_op jit(solution)/shard_map/ppermute | solution.py:14
  194.0 8.2 %fusion.21 = (f32[64,128,128]{1,2,0:T(8,128)}, f32[64,128,128]{1,2,0:T(8,128)}, f32[64,128,128]{1,2,0:T(8,128)}) fusion(f32[64,1,128,128]{2,3,0,1:T(8,128)S(1)} %copy-done.2, f32[64,1,128,128]{2,3,0,1:T(8,128)S(1)} %copy-done.1, f32[64,1,128,128]{2,3,0,1:T(8,128)S(1)} %copy-done, f32[128,128]{0,1:T(8,128)S(1)} %copy.28, f32[128,128]{0,1:T(8,128)S(1)} %copy.26, ...), kind=kLoop, calls=%fused_computation.37 | loop fusion | flops 25165824 | bytes 31719424 | tf_op jit(solution)/shard_map/add | solution.py:65
  202.2 18.0 %fusion.13 = f32[2,192,128,128]{2,3,0,1:T(8,128)} fusion(f32[64,128,128]{1,2,0:T(8,128)} %get-tuple-element.15, f32[64,128,128]{1,2,0:T(8,128)} %get-tuple-element.14, f32[64,128,128]{1,2,0:T(8,128)} %get-tuple-element.13, f32[1,128,128]{2,1,0:T(8,128)S(1)} %get-tuple-element.26, f32[1,128,128]{2,1,0:T(8,128)S(1)} %get-tuple-element.27), kind=kOutput, calls=%fused_computation.20 | convolution fusion | flops 4838162432 | bytes 37879808 | tf_op jit(solution)/shard_map/xca,mab->xmcb/dot_general | solution.py:31
  220.2 19.8 %multiply_add_fusion = (f32[1,192,128,128]{2,3,0,1:T(8,128)}, f32[1,192,128,128]{2,3,0,1:T(8,128)}) fusion(f32[2,192,128,128]{2,3,0,1:T(8,128)} %fusion.13, f32[128,128]{0,1:T(8,128)S(1)} %get-tuple-element.28, f32[128,128]{0,1:T(8,128)S(1)} %get-tuple-element.29), kind=kLoop, calls=%fused_computation.19 | loop fusion | flops 18874368 | bytes 50462720 | tf_op jit(solution)/shard_map/add | solution.py:36
  240.0 16.6 %fusion.17 = f32[2,64,192,128]{3,1,2,0:T(8,128)} fusion(f32[1,192,128,128]{2,3,0,1:T(8,128)} %get-tuple-element.6, f32[1,192,128,128]{2,3,0,1:T(8,128)} %get-tuple-element.5, f32[1,64,2,128]{3,1,2,0:T(8,128)S(1)} %get-tuple-element.25, f32[1,64,2,128]{3,1,2,0:T(8,128)S(1)} %get-tuple-element.24), kind=kOutput, calls=%fused_computation.33 | convolution fusion | flops 4838162432 | bytes 37879808 | tf_op jit(solution)/shard_map/yqxb,xmcb->yqmc/dot_general | solution.py:42
  256.6 9.0 %fusion.5 = bf16[2,64,256,128]{3,1,2,0:T(8,128)(2,1)} fusion(f32[2,64,192,128]{3,1,2,0:T(8,128)} %fusion.17, f32[2,64,64,128]{3,1,2,0:T(8,128)S(1)} %copy-done.3, f32[256]{0:T(256)S(1)} %mul.388), kind=kLoop, calls=%fused_computation.7 | loop fusion | flops 12582912 | bytes 25166848 | tf_op jit(solution)/shard_map/convert_element_type | solution.py:75
  265.6 12.0 %copy.33 = bf16[2,64,256,128]{3,2,0,1:T(8,128)(2,1)} copy(bf16[2,64,256,128]{3,1,2,0:T(8,128)(2,1)} %fusion.5) | data formatting | bytes 16777216 | tf_op jit(solution)/shard_map/convert_element_type | solution.py:75
  277.6 110.1 %all_to_all.5 = bf16[2,64,256,128]{3,2,0,1:T(8,128)(2,1)S(1)} all-to-all(bf16[2,64,256,128]{3,2,0,1:T(8,128)(2,1)} %copy.33), channel_id=1, replica_groups=mesh['inp'=8,'tm'=8,'bl'=2] {'inp','tm'}, dimensions={1} | all-to-all | bytes 16777216 | tf_op jit(solution)/shard_map/all_to_all | solution.py:76
  387.8 7.3 %copy.53 = bf16[2,8,8,4,64,128]{5,3,2,0,4,1:T(4,128)(2,1)} copy(bf16[2,8,8,4,64,128]{5,4,3,0,2,1:T(8,128)(2,1)S(1)} %bitcast.154) | data formatting | bytes 16777216 | tf_op jit(solution)/shard_map/reshape | solution.py:80
  395.1 14.4 %reshape.241 = bf16[8,64,8192]{2,1,0:T(8,128)(2,1)} reshape(bf16[8,64,2,8,4,128]{5,4,3,2,1,0:T(4,128)(2,1)} %bitcast.151) | data formatting | bytes 16777216 | tf_op jit(solution)/shard_map/reshape | solution.py:81
  409.5 0.2 compare_convert_fusion
  409.7 15.1 %stack_reshape.3 = bf16[1,8,64,8192]{3,2,1,0:T(8,128)(2,1)} reshape(bf16[8,64,2,8,4,128]{5,4,3,2,1,0:T(4,128)(2,1)} %bitcast.152) | data formatting | bytes 16777216 | tf_op jit(solution)/shard_map/stack;reshape | solution.py:87
  424.9 8.2 %fusion.78 = (bf16[8,64,4096]{2,1,0:T(8,128)(2,1)}, bf16[8,64,4096]{2,1,0:T(8,128)(2,1)}) fusion(bf16[8,64,8192]{2,1,0:T(8,128)(2,1)} %reshape.241), kind=kLoop, calls=%fused_computation.129 | loop fusion | flops 2097152 | bytes 16777216 | tf_op jit(solution)/shard_map/slice | solution.py:83
  433.1 7.9 %maximum_bitcast_fusion.8 = bf16[1,8,64,8192]{3,2,1,0:T(8,128)(2,1)} fusion(bf16[8,64,4096]{2,1,0:T(8,128)(2,1)} %get-tuple-element.19, bf16[8,64,4096]{2,1,0:T(8,128)(2,1)} %get-tuple-element.18), kind=kLoop, calls=%fused_computation.25 | loop fusion | flops 16777216 | bytes 16777216 | tf_op jit(solution)/shard_map/stack | solution.py:87
  440.9 13.8 %pad_maximum_fusion = bf16[2,8,64,8192]{3,2,1,0:T(8,128)(2,1)} fusion(bf16[1,8,64,8192]{3,2,1,0:T(8,128)(2,1)} %maximum_bitcast_fusion.8, bf16[1,8,64,8192]{3,2,1,0:T(8,128)(2,1)} %stack_reshape.3), kind=kLoop, calls=%fused_computation.8 | loop fusion | flops 8388608 | bytes 33554432 | tf_op jit(solution)/shard_map/stack | solution.py:87
  454.7 42.5 %broadcast_multiply_fusion = f32[2,2,8,64,1024]{4,3,2,1,0:T(8,128)} fusion(bf16[1024,8192,1,1,1]{1,0,4,3,2:T(8,128)(2,1)} %bitcast.160, bf16[2,8192]{1,0:T(2,128)(2,1)S(1)} %compare_convert_fusion, bf16[2,8,64,8192]{3,2,1,0:T(8,128)(2,1)} %pad_maximum_fusion), kind=kOutput, calls=%fused_computation.60 | convolution fusion | flops 34378612736 | bytes 41975808 | tf_op jit(solution)/shard_map/xgpik,qk->xgpiq/dot_general | solution.py:90
  (28 shorter events, 1.0 us)
Async XLA Ops:
  6.5 448.2 %all-gather.2.cloned.1.call-start = ((), (), s32[]{:S(2)}) async-start(), calls=%async_computation.1 | async-start | bytes 25165824 | tf_op jit(solution)/shard_map/all_gather | solution.py:88
  54.0 140.0 %collective-permute-start = (bf16[64,3,128,128]{2,3,0,1:T(8,128)(2,1)}, bf16[64,3,128,128]{2,3,0,1:T(8,128)(2,1)}, u32[]{:S(2)}, u32[]{:S(2)}) collective-permute-start(bf16[64,3,128,128]{2,3,0,1:T(8,128)(2,1)} %copy.49), channel_id=1, source_target_pairs={{2,0},{4,2},{6,4},{8,6},{10,8},{12,10},{14,12},{3,1},{5,3},{7,5},{... | collective-permute-start | bytes 18874376 | tf_op jit(solution)/shard_map/ppermute | solution.py:14
  91.5 5.6 %copy-start.4 = (f32[4,16384]{1,0:T(4,128)S(1)}, f32[4,16384]{1,0:T(4,128)}, u32[]{:S(2)}) copy-start(f32[4,16384]{1,0:T(4,128)} %param.4) | copy-start | bytes 786436
  91.5 6.2 %copy-start.5 = (s32[64]{0:T(128)S(1)}, s32[64]{0:T(128)}, u32[]{:S(2)}) copy-start(s32[64]{0:T(128)} %param.5) | copy-start | bytes 772
  107.9 86.1 %copy-start = (f32[64,1,128,128]{2,3,0,1:T(8,128)S(1)}, f32[64,1,128,128]{2,3,0,1:T(8,128)}, u32[]{:S(2)}) copy-start(f32[64,1,128,128]{2,3,0,1:T(8,128)} %copy.46) | copy-start | bytes 12582916
  107.9 86.1 %copy-start.1 = (f32[64,1,128,128]{2,3,0,1:T(8,128)S(1)}, f32[64,1,128,128]{2,3,0,1:T(8,128)}, u32[]{:S(2)}) copy-start(f32[64,1,128,128]{2,3,0,1:T(8,128)} %copy.47) | copy-start | bytes 12582916
  107.9 86.0 %copy-start.2 = (f32[64,1,128,128]{2,3,0,1:T(8,128)S(1)}, f32[64,1,128,128]{2,3,0,1:T(8,128)}, u32[]{:S(2)}) copy-start(f32[64,1,128,128]{2,3,0,1:T(8,128)} %copy.48) | copy-start | bytes 12582916
  240.0 16.6 %copy-start.3 = (f32[2,64,64,128]{3,1,2,0:T(8,128)S(1)}, f32[2,64,64,128]{3,1,2,0:T(8,128)}, u32[]{:S(2)}) copy-start(f32[2,64,64,128]{3,1,2,0:T(8,128)} %fusion.40) | copy-start | bytes 12582916
Sparse Core Ops, SparseCore 0:
  409.6 29.6 all-gather.1
where the time goes:
time: 509 us; the launch traced here: 504 us
  local copies, waits for them, and re-layouts  113 us (22%)
  blocking collectives  110 us (22%)
  other arithmetic  90.9 us (18%)
  matrix products  89.4 us (18%)
  waiting for transfers between devices  81.7 us (16%)
  between operations  13.8 us (3%)
  starting transfers between devices  5.18 us (1%)
    all_to_all x1, blocking collectives, shards(): lax.all_to_all(spectra, ('inp', 'tm'), split_axis=1, concat_axis=1, tiled...  110 us
    ppermute x1, waiting for transfers between devices, passed_along(): lax.ppermute(value, axis, [(source, source + steps) for source in range(i...  81.6 us
    unnamed x19, local copies, waits for them, and re-layouts  49.5 us
    dot_general x1, matrix products, shards(): jnp.einsum('xgpik,qk->xgpiq', lhs, columns, preferred_element_type=jnp.fl...  42.5 us
    dot_general x2, matrix products, transform(): jnp.einsum('xca,mab->xmcb', table_one, blocks, precision=precision)  26 us
    unnamed x1, other arithmetic  21.8 us
    another operation x2, other arithmetic, shards(): lhs = jnp.stack([own, swapped])[:, None] * mask[None, :, None, None, :]  21.6 us
    dot_general x2, matrix products, transform(): jnp.einsum('yqxb,xmcb->yqmc', table_two, twisted, precision=precision)  21 us
  transfers between devices with their start and end apart: 2, of which 1 were waited for; matrix products, arithmetic and copies ran while one was open for 19% of the time, Pallas kernels for 0%

commit v1 on v0

--- a/solution.py
+++ b/solution.py
@@ -73,7 +73,14 @@
     both_parts = jnp.concatenate([first_part, second_part], axis=2)
     scale = jnp.tile(flags.astype(jnp.float32) / (8.0 * math.sqrt(length)), spectra_dev)
     spectra = (both_parts * scale[None, None, :, None]).astype(jnp.bfloat16)
-    turned = lax.all_to_all(spectra, ("inp", "tm"), split_axis=1, concat_axis=1, tiled=True)
+
+    def _balance_target(base_x):
+        b_next = lax.all_to_all(
+            jnp.stack(jnp.split(base_x, lax.axis_size(("inp", "tm")), axis=1)), ("inp", "tm"), 0, 0
+        )
+        return jnp.concatenate(b_next, axis=1)
+
+    turned = _balance_target(spectra)
     groups_inp = lax.axis_size("inp")
     groups_tm = lax.axis_size("tm")
     out_groups = FIRST // CH_AVG

time: 509 us -> 537 us (1.055)
  local copies, waits for them, and re-layouts: 113 us -> 130 us
  other arithmetic: 90.9 us -> 104 us
    unnamed x19 -> x71, local copies, waits for them, and re-layouts: 49.5 us -> 20.3 us
    slice x1 -> x5, local copies, waits for them, and re-layouts: 6.02 us -> 28.7 us  [shards(): own_pieces = [samples[:, j] for j in range(spectra_dev)]]
    split x0 -> x4, local copies, waits for them, and re-layouts: none -> 18 us  [_balance_target(): jnp.split(base_x, lax.axis_size(('inp', 'tm')), axis=1)]
    convert_element_type x0 -> x1, other arithmetic: none -> 7.99 us  [shards(): next_pieces = [following[:, j].astype(jnp.float32) for j in range(reach)]]
    reshape x1 -> x0, local copies, waits for them, and re-layouts: 7.28 us -> none  [shards(): rows = turned.reshape(2, groups_inp, groups_tm, spectra_dev, inputs, FIRST)]
    transpose x0 -> x1, local copies, waits for them, and re-layouts: none -> 7.28 us  [shards(): jnp.transpose(rows, (1, 4, 0, 2, 3, 5)).reshape(groups_inp, inputs, -1)]
    add x1, other arithmetic: 8.21 us -> 14.5 us  [filtered(): total = total + tap_blocks[offset][None] * pieces[spectrum + offset]]
    convert_element_type x1 -> x3, local copies, waits for them, and re-layouts: 12 us -> 16.9 us  [shards(): next_pieces = [following[:, j].astype(jnp.float32) for j in range(reach)]]
where the time goes in v1:
time: 537 us; the launch traced here: 533 us
  local copies, waits for them, and re-layouts  130 us (24%)
  blocking collectives  110 us (20%)
  other arithmetic  104 us (19%)
  matrix products  89 us (17%)
  waiting for transfers between devices  81 us (15%)
  between operations  14.2 us (3%)
    all_to_all x1, blocking collectives, _balance_target(): lax.all_to_all(jnp.stack(jnp.split(base_x, lax.axis_size(('inp', 'tm')),...  110 us
    ppermute x1, waiting for transfers between devices, passed_along(): lax.ppermute(value, axis, [(source, source + steps) for source in range(i...  80.9 us
    dot_general x1, matrix products, shards(): jnp.einsum('xgpik,qk->xgpiq', lhs, columns, preferred_element_type=jnp.fl...  42.5 us
    slice x5, local copies, waits for them, and re-layouts, shards(): own_pieces = [samples[:, j] for j in range(spectra_dev)]  28.7 us
    dot_general x2, matrix products, transform(): jnp.einsum('xca,mab->xmcb', table_one, blocks, precision=precision)  25.4 us
    unnamed x1, other arithmetic  21.8 us
    another operation x2, other arithmetic, shards(): lhs = jnp.stack([own, swapped])[:, None] * mask[None, :, None, None, :]  21.6 us
    add x2, other arithmetic, transform(): real_one * cos_twist + imag_one * sin_twist  21.6 us
  transfers between devices with their start and end apart: 2, of which 1 were waited for; matrix products, arithmetic and copies ran while one was open for 19% of the time, Pallas kernels for 0%

profile of v1, /device:TPU:2, one launch (start us, length us, event | category | flops | bytes accessed | tf_op | source)
XLA Modules:
  0.0 532.6 jit_solution(14981294532154656845)
XLA Ops:
  6.5 21.8 %convert_bitcast_fusion = (f32[8,8,512,128]{3,1,2,0:T(8,128)}, bf16[8,8,512,128]{3,1,2,0:T(8,128)(2,1)}) fusion(s32[64,65536]{1,0:T(8,128)} %param.3), kind=kLoop, calls=%fused_computation.9 | loop fusion | flops 8388608 | bytes 41943040
  28.3 9.0 %copy.1948 = bf16[8,8,512,128]{3,2,1,0:T(8,128)(2,1)} copy(bf16[8,8,512,128]{3,1,2,0:T(8,128)(2,1)} %get-tuple-element.12) | data formatting | bytes 16777216
  37.3 8.2 %slice.95 = bf16[64,3,128,128]{3,2,1,0:T(8,128)(2,1)} slice(bf16[64,4,128,128]{3,2,1,0:T(8,128)(2,1)} %bitcast.288), slice={[0:64], [0:3], [0:128], [0:128]} | slice | bytes 12582912 | tf_op jit(solution)/shard_map/slice | solution.py:55
  45.5 5.2 collective-permute-start
  51.4 9.4 %copy.1947 = f32[8,8,512,128]{3,2,1,0:T(8,128)S(1)} copy(f32[8,8,512,128]{3,1,2,0:T(8,128)} %get-tuple-element.11) | data formatting | bytes 33554432
  60.8 6.2 %fusion.77 = (f32[64,1,128,128]{3,2,1,0:T(8,128)}, f32[64,1,128,128]{3,2,1,0:T(8,128)}, f32[64,1,128,128]{3,2,1,0:T(8,128)}, f32[64,1,128,128]{3,2,1,0:T(8,128)}) fusion(f32[64,4,128,128]{3,2,1,0:T(8,128)S(1)} %bitcast.286), kind=kLoop, calls=%fused_computation.191 | loop fusion | bytes 33554432 | tf_op jit(solution)/shard_map/slice | solution.py:69
  66.9 5.6 %copy.1859 = f32[64,1,128,128]{2,3,0,1:T(8,128)} copy(f32[64,1,128,128]{3,2,1,0:T(8,128)} %get-tuple-element.7) | data formatting | bytes 8388608 | tf_op jit(solution)/shard_map/slice | solution.py:69
  72.5 5.6 %copy.1865 = f32[64,1,128,128]{2,3,0,1:T(8,128)} copy(f32[64,1,128,128]{3,2,1,0:T(8,128)} %get-tuple-element.8) | data formatting | bytes 8388608 | tf_op jit(solution)/shard_map/slice | solution.py:69
  78.2 5.6 %copy.1863 = f32[64,1,128,128]{2,3,0,1:T(8,128)} copy(f32[64,1,128,128]{3,2,1,0:T(8,128)} %get-tuple-element.9) | data formatting | bytes 8388608 | tf_op jit(solution)/shard_map/slice | solution.py:69
  83.8 5.7 %copy.1861 = f32[64,1,128,128]{2,3,0,1:T(8,128)} copy(f32[64,1,128,128]{3,2,1,0:T(8,128)} %get-tuple-element.10) | data formatting | bytes 8388608 | tf_op jit(solution)/shard_map/slice | solution.py:69
  90.3 7.9 %fusion.37 = f32[2,64,128,128]{2,3,0,1:T(8,128)S(1)} fusion(f32[64,1,128,128]{2,3,0,1:T(8,128)} %copy.1865, f32[64,1,128,128]{2,3,0,1:T(8,128)} %copy.1863, f32[64,1,128,128]{2,3,0,1:T(8,128)} %copy.1861, f32[64,1,128,128]{2,3,0,1:T(8,128)} %copy.1859, f32[128,128]{0,1:T(8,128)S(1)} %copy.1864, f32[128,128]{0,1:T(8,128)S(1)} %copy.1862, ...), kind=kOutput, calls=%fused_computation.62 | convolution fusion | flops 1617985536 | bytes 25559040 | tf_op jit(solution)/shard_map/xca,mab->xmcb/dot_general | solution.py:31
  104.5 80.9 %collective-permute-done = bf16[64,3,128,128]{3,2,1,0:T(8,128)(2,1)} collective-permute-done((bf16[64,3,128,128]{3,2,1,0:T(8,128)(2,1)}, bf16[64,3,128,128]{3,2,1,0:T(8,128)(2,1)}, u32[]{:S(2)}, u32[]{:S(2)}) %collective-permute-start) | collective-permute-done | bytes 6291488 | tf_op jit(solution)/shard_map/ppermute | solution.py:14
  185.4 8.0 %slice_convert_fusion.2 = (f32[64,1,128,128]{3,2,1,0:T(8,128)}, f32[64,1,128,128]{3,2,1,0:T(8,128)}, f32[64,1,128,128]{3,2,1,0:T(8,128)}) fusion(bf16[64,3,128,128]{3,2,1,0:T(8,128)(2,1)} %collective-permute-done), kind=kLoop, calls=%fused_computation.66 | loop fusion | flops 3145728 | bytes 18874368 | tf_op jit(solution)/shard_map/convert_element_type | solution.py:70
  193.4 5.7 %copy.1867 = f32[64,1,128,128]{2,3,0,1:T(8,128)} copy(f32[64,1,128,128]{3,2,1,0:T(8,128)} %get-tuple-element.84) | data formatting | bytes 8388608 | tf_op jit(solution)/shard_map/convert_element_type | solution.py:70
  199.1 5.6 %copy.1869 = f32[64,1,128,128]{2,3,0,1:T(8,128)} copy(f32[64,1,128,128]{3,2,1,0:T(8,128)} %get-tuple-element.85) | data formatting | bytes 8388608 | tf_op jit(solution)/shard_map/convert_element_type | solution.py:70
  204.7 5.6 %copy.1868 = f32[64,1,128,128]{2,3,0,1:T(8,128)} copy(f32[64,1,128,128]{3,2,1,0:T(8,128)} %get-tuple-element.86) | data formatting | bytes 8388608 | tf_op jit(solution)/shard_map/convert_element_type | solution.py:70
  210.3 14.5 %fusion.23 = (f32[64,128,128]{1,2,0:T(8,128)}, f32[64,128,128]{1,2,0:T(8,128)}, f32[64,128,128]{1,2,0:T(8,128)}) fusion(f32[64,1,128,128]{2,3,0,1:T(8,128)} %copy.1867, f32[64,1,128,128]{2,3,0,1:T(8,128)} %copy.1865, f32[64,1,128,128]{2,3,0,1:T(8,128)} %copy.1863, f32[64,1,128,128]{2,3,0,1:T(8,128)} %copy.1861, f32[128,128]{0,1:T(8,128)S(1)} %copy.1864, ...), kind=kLoop, calls=%fused_computation.40 | loop fusion | flops 22020096 | bytes 38010880 | tf_op jit(solution)/shard_map/add | solution.py:65
  224.8 17.5 %fusion.13 = f32[2,192,128,128]{2,3,0,1:T(8,128)} fusion(f32[64,128,128]{1,2,0:T(8,128)} %get-tuple-element.15, f32[64,128,128]{1,2,0:T(8,128)} %get-tuple-element.14, f32[64,128,128]{1,2,0:T(8,128)} %get-tuple-element.13, f32[1,128,128]{2,1,0:T(8,128)S(1)} %get-tuple-element.93, f32[1,128,128]{2,1,0:T(8,128)S(1)} %get-tuple-element.94), kind=kOutput, calls=%fused_computation.20 | convolution fusion | flops 4838162432 | bytes 37879808 | tf_op jit(solution)/shard_map/xca,mab->xmcb/dot_general | solution.py:31
  242.3 19.7 %multiply_add_fusion = (f32[1,192,128,128]{2,3,0,1:T(8,128)}, f32[1,192,128,128]{2,3,0,1:T(8,128)}) fusion(f32[2,192,128,128]{2,3,0,1:T(8,128)} %fusion.13, f32[128,128]{0,1:T(8,128)S(1)} %get-tuple-element.95, f32[128,128]{0,1:T(8,128)S(1)} %get-tuple-element.96), kind=kLoop, calls=%fused_computation.19 | loop fusion | flops 18874368 | bytes 50462720 | tf_op jit(solution)/shard_map/add | solution.py:36
  262.0 16.8 %fusion.17 = f32[2,64,192,128]{3,1,2,0:T(8,128)} fusion(f32[1,192,128,128]{2,3,0,1:T(8,128)} %get-tuple-element.6, f32[1,192,128,128]{2,3,0,1:T(8,128)} %get-tuple-element.5, f32[1,64,2,128]{3,1,2,0:T(8,128)S(1)} %get-tuple-element.92, f32[1,64,2,128]{3,1,2,0:T(8,128)S(1)} %get-tuple-element.91), kind=kOutput, calls=%fused_computation.27 | convolution fusion | flops 4838162432 | bytes 37879808 | tf_op jit(solution)/shard_map/yqxb,xmcb->yqmc/dot_general | solution.py:42
  278.8 6.8 %fusion.5 = bf16[2,64,256,128]{3,1,2,0:T(8,128)(2,1)S(1)} fusion(f32[2,64,192,128]{3,1,2,0:T(8,128)} %fusion.17, f32[2,64,64,128]{3,1,2,0:T(8,128)S(1)} %copy-done, f32[256]{0:T(256)S(1)} %mul.388), kind=kLoop, calls=%fused_computation.7 | loop fusion | flops 12582912 | bytes 25166848 | tf_op jit(solution)/shard_map/convert_element_type | solution.py:75
  287.4 5.3 fusion.81
  292.7 5.6 %fusion.79 = (bf16[2,1,256,128]{3,1,2,0:T(2,128)(2,1)S(1)}, bf16[2,1,256,128]{3,1,2,0:T(2,128)(2,1)S(1)}, bf16[2,1,256,128]{3,1,2,0:T(2,128)(2,1)S(1)}, bf16[2,1...) fusion(bf16[2,64,256,128]{3,1,2,0:T(8,128)(2,1)S(1)} %fusion.5), kind=kLoop, calls=%fused_computation.193 | loop fusion | bytes 4980736 | tf_op jit(solution)/shard_map/split | solution.py:79
  298.3 5.3 fusion.80
  306.0 109.9 %all_to_all.5 = bf16[64,2,1,256,128]{4,3,1,2,0:T(8,128)(2,1)S(1)} all-to-all(bf16[64,2,1,256,128]{4,3,1,2,0:T(8,128)(2,1)S(1)} %constant_dynamic-update-slice_fusion), channel_id=1, replica_groups=mesh['inp'=8,'tm'=8,'bl'=2] {'inp','tm'}, dimensions={0} | all-to-all | bytes 16777216 | tf_op jit(solution)/shard_map/all_to_all | solution.py:78
  415.9 7.3 %copy.1871 = bf16[8,64,2,8,4,128]{5,4,3,2,1,0:T(4,128)(2,1)} copy(bf16[8,64,2,8,4,128]{5,1,4,2,3,0:T(8,128)(2,1)S(1)} %bitcast.287) | data formatting | bytes 16777216 | tf_op jit(solution)/shard_map/transpose | solution.py:88
  423.2 14.4 %reshape.241 = bf16[8,64,8192]{2,1,0:T(8,128)(2,1)} reshape(bf16[8,64,2,8,4,128]{5,4,3,2,1,0:T(4,128)(2,1)} %copy.1871) | data formatting | bytes 16777216 | tf_op jit(solution)/shard_map/reshape | solution.py:88
  437.9 15.2 %stack_reshape.3 = bf16[1,8,64,8192]{3,2,1,0:T(8,128)(2,1)} reshape(bf16[8,64,2,8,4,128]{5,4,3,2,1,0:T(4,128)(2,1)} %copy.1871) | data formatting | bytes 16777216 | tf_op jit(solution)/shard_map/stack;reshape | solution.py:94
  453.0 8.4 %fusion.78 = (bf16[8,64,4096]{2,1,0:T(8,128)(2,1)}, bf16[8,64,4096]{2,1,0:T(8,128)(2,1)}) fusion(bf16[8,64,8192]{2,1,0:T(8,128)(2,1)} %reshape.241), kind=kLoop, calls=%fused_computation.192 | loop fusion | flops 2097152 | bytes 16777216 | tf_op jit(solution)/shard_map/slice | solution.py:90
  461.4 7.9 %maximum_bitcast_fusion.8 = bf16[1,8,64,8192]{3,2,1,0:T(8,128)(2,1)} fusion(bf16[8,64,4096]{2,1,0:T(8,128)(2,1)} %get-tuple-element.19, bf16[8,64,4096]{2,1,0:T(8,128)(2,1)} %get-tuple-element.18), kind=kLoop, calls=%fused_computation.25 | loop fusion | flops 16777216 | bytes 16777216 | tf_op jit(solution)/shard_map/stack | solution.py:94
  469.3 13.8 %pad_maximum_fusion = bf16[2,8,64,8192]{3,2,1,0:T(8,128)(2,1)} fusion(bf16[1,8,64,8192]{3,2,1,0:T(8,128)(2,1)} %maximum_bitcast_fusion.8, bf16[1,8,64,8192]{3,2,1,0:T(8,128)(2,1)} %stack_reshape.3), kind=kLoop, calls=%fused_computation.8 | loop fusion | flops 8388608 | bytes 33554432 | tf_op jit(solution)/shard_map/stack | solution.py:94
  483.1 42.5 %broadcast_multiply_fusion = f32[2,2,8,64,1024]{4,3,2,1,0:T(8,128)} fusion(bf16[1024,8192,1,1,1]{1,0,4,3,2:T(8,128)(2,1)} %bitcast.293, bf16[2,8192]{1,0:T(2,128)(2,1)S(1)} %compare_convert_fusion, bf16[2,8,64,8192]{3,2,1,0:T(8,128)(2,1)} %pad_maximum_fusion), kind=kOutput, calls=%fused_computation.59 | convolution fusion | flops 34378612736 | bytes 41975808 | tf_op jit(solution)/shard_map/xgpik,qk->xgpiq/dot_general | solution.py:97
  (92 shorter events, 11.8 us)
Async XLA Ops:
  6.5 476.5 %all-gather.2.cloned.1.call-start = ((), (), s32[]{:S(2)}) async-start(), calls=%async_computation.1 | async-start | bytes 25165824 | tf_op jit(solution)/shard_map/all_gather | solution.py:95
  37.3 13.4 %copy-start.2 = (s32[64]{0:T(128)S(1)}, s32[64]{0:T(128)}, u32[]{:S(2)}) copy-start(s32[64]{0:T(128)} %param.5) | copy-start | bytes 772
  37.3 13.5 %copy-start.1 = (f32[4,16384]{1,0:T(4,128)S(1)}, f32[4,16384]{1,0:T(4,128)}, u32[]{:S(2)}) copy-start(f32[4,16384]{1,0:T(4,128)} %param.4) | copy-start | bytes 786436
  45.5 140.0 %collective-permute-start = (bf16[64,3,128,128]{3,2,1,0:T(8,128)(2,1)}, bf16[64,3,128,128]{3,2,1,0:T(8,128)(2,1)}, u32[]{:S(2)}, u32[]{:S(2)}) collective-permute-start(bf16[64,3,128,128]{3,2,1,0:T(8,128)(2,1)} %slice.95), channel_id=1, source_target_pairs={{2,0},{4,2},{6,4},{8,6},{10,8},{12,10},{14,12},{3,1},{5,3},{7,5},{... | collective-permute-start | bytes 18874376 | tf_op jit(solution)/shard_map/ppermute | solution.py:14
  262.0 16.8 %copy-start = (f32[2,64,64,128]{3,1,2,0:T(8,128)S(1)}, f32[2,64,64,128]{3,1,2,0:T(8,128)}, u32[]{:S(2)}) copy-start(f32[2,64,64,128]{3,1,2,0:T(8,128)} %fusion.40) | copy-start | bytes 12582916
Sparse Core Ops, SparseCore 0:
  437.7 30.0 all-gather.1
